TPU v7x, 32 devices: a whole 2x2x4 slice. The times are simulated.
32 devices in a mesh: dp: 4 (over x, core), seq: 4 (over z), chan: 2 (over y).
Axes of the slice: x: 2, y: 2, z: 4, core: 2. Of those that a mesh axis runs over, the one named last changes fastest.
Arguments:
- inputs: bfloat16 [4, 8, 256, 2048], P('dp', 'seq', None, 'chan'), may hold values from -6 to 6
- cotangent: bfloat16 [4, 8, 256, 2048], P('dp', 'seq', None, 'chan'), may hold values from -6 to 6
- rows_in: bfloat16 [256, 256], replicated, may hold values from -0.375 to 0.375
- cols_mix: bfloat16 [8, 8], replicated, may hold values from -2 to 2
- blocks_gate: bfloat16 [4, 512, 512], P('chan'), may hold values from -0.25 to 0.25
- blocks_up: bfloat16 [4, 512, 512], P('chan'), may hold values from -0.25 to 0.25
- mix_gate: bfloat16 [4, 4, 512], replicated, may hold values from -3 to 3
- mix_up: bfloat16 [4, 4, 512], replicated, may hold values from -3 to 3
Outputs:
- input_grad: bfloat16 [4, 8, 256, 2048], P('dp', 'seq', None, 'chan')
- rows_grad: float32 [256, 256], replicated
- cols_grad: float32 [8, 8], replicated
- blocks_gate_grad: float32 [4, 512, 512], P('chan')
- blocks_up_grad: float32 [4, 512, 512], P('chan')
- mix_gate_grad: float32 [4, 4, 512], P(None, 'chan')
- mix_up_grad: float32 [4, 4, 512], P(None, 'chan')
All inputs are finite; a program needn't handle non-finite values.
Results may differ from a plain program's by a relative error of at most 0.011.
Values may be sent and summed in bfloat16 or wider, within the bound.
No kernel may reach another device: no remote copies, remote signals or barrier semaphores. Data moves between devices by JAX's collectives and lax.ppermute only.
A program may use at most 128 MiB of HBM per device.

v0:
```python
import math
import jax
import jax.numpy as jnp
from jax import lax
from jax.sharding import PartitionSpec as P


def column_keep(segment, cols_mix):
    mixed = jnp.einsum(
        "er,brcd->becd", cols_mix, segment, preferred_element_type=jnp.float32
    ).astype(jnp.bfloat16)
    return (segment, mixed)


def body(inputs, cotangent, rows_in, cols_mix, blocks_gate, blocks_up, mix_gate, mix_up):
    batch_dev, rows_dev, cols_all, width_dev = inputs.shape
    block_size = blocks_gate.shape[1]
    local_blocks = blocks_gate.shape[0]
    chan_index = lax.axis_index("chan")
    split_shape = (batch_dev, rows_dev, cols_all, local_blocks, block_size)
    first = jnp.einsum("ec,brcd->bred", rows_in, inputs, preferred_element_type=jnp.float32).astype(
        jnp.bfloat16
    )
    first_cols, second_cols = column_keep(
        lax.all_to_all(first, "seq", split_axis=2, concat_axis=1, tiled=True), cols_mix
    )
    second_rows = lax.all_to_all(second_cols, "seq", split_axis=1, concat_axis=2, tiled=True)
    hidden = (inputs.astype(jnp.float32) + second_rows.astype(jnp.float32)).astype(jnp.bfloat16)
    hidden_blocks = hidden.reshape(split_shape)
    gate_rows_own = lax.dynamic_slice_in_dim(
        mix_gate, chan_index * local_blocks, local_blocks, 0
    ).astype(jnp.float32)
    up_rows_own = lax.dynamic_slice_in_dim(
        mix_up, chan_index * local_blocks, local_blocks, 0
    ).astype(jnp.float32)
    gate_mid = jnp.einsum(
        "brckj,kjl->brckl", hidden_blocks, blocks_gate, preferred_element_type=jnp.float32
    ).astype(jnp.bfloat16)
    up_mid = jnp.einsum(
        "brckj,kjl->brckl", hidden_blocks, blocks_up, preferred_element_type=jnp.float32
    ).astype(jnp.bfloat16)
    gate_add = jnp.einsum(
        "mkj,brckj->brcmj",
        gate_rows_own,
        lax.all_gather(gate_mid, "chan", axis=3, tiled=True).astype(jnp.float32),
    )
    up_add = jnp.einsum(
        "mkj,brckj->brcmj",
        up_rows_own,
        lax.all_gather(up_mid, "chan", axis=3, tiled=True).astype(jnp.float32),
    )
    upstream = cotangent.astype(jnp.float32).reshape(split_shape)
    sigma = jax.nn.sigmoid(gate_add)
    up_grad = (upstream * gate_add * sigma).astype(jnp.bfloat16)
    gate_grad = (upstream * up_add * sigma * (1.0 + gate_add * (1.0 - sigma))).astype(jnp.bfloat16)
    gate_all, up_all = (
        lax.all_gather(gate_grad, "chan", axis=3, tiled=True),
        lax.all_gather(up_grad, "chan", axis=3, tiled=True),
    )
    gate_cols_own = lax.dynamic_slice_in_dim(
        mix_gate, chan_index * local_blocks, local_blocks, 1
    ).astype(jnp.float32)
    up_cols_own = lax.dynamic_slice_in_dim(
        mix_up, chan_index * local_blocks, local_blocks, 1
    ).astype(jnp.float32)
    mix_gate_sum = jnp.einsum(
        "brcmj,brckj->mkj", gate_all, gate_mid, preferred_element_type=jnp.float32
    )
    mix_up_sum = jnp.einsum("brcmj,brckj->mkj", up_all, up_mid, preferred_element_type=jnp.float32)
    gate_back = jnp.einsum("mkj,brcmj->brckj", gate_cols_own, gate_all.astype(jnp.float32)).astype(
        jnp.bfloat16
    )
    up_back = jnp.einsum("mkj,brcmj->brckj", up_cols_own, up_all.astype(jnp.float32)).astype(
        jnp.bfloat16
    )
    blocks_gate_sum = jnp.einsum(
        "brckj,brckl->kjl", hidden_blocks, gate_back, preferred_element_type=jnp.float32
    )
    blocks_up_sum = jnp.einsum(
        "brckj,brckl->kjl", hidden_blocks, up_back, preferred_element_type=jnp.float32
    )
    hidden_grad = (
        upstream
        + jnp.einsum("brckl,kjl->brckj", gate_back, blocks_gate, preferred_element_type=jnp.float32)
        + jnp.einsum("brckl,kjl->brckj", up_back, blocks_up, preferred_element_type=jnp.float32)
    )
    hidden_grad = hidden_grad.reshape(inputs.shape).astype(jnp.bfloat16)
    segment = lax.all_to_all(hidden_grad, "seq", split_axis=2, concat_axis=1, tiled=True)
    mixed = jnp.einsum(
        "er,becd->brcd", cols_mix, segment, preferred_element_type=jnp.float32
    ).astype(jnp.bfloat16)
    cols_sum = jnp.einsum("becd,brcd->er", segment, first_cols, preferred_element_type=jnp.float32)
    first_grad = lax.all_to_all(mixed, "seq", split_axis=1, concat_axis=2, tiled=True)
    rows_sum = jnp.einsum("bred,brcd->ec", first_grad, inputs, preferred_element_type=jnp.float32)
    input_grad = (
        hidden_grad.astype(jnp.float32)
        + jnp.einsum("ec,bred->brcd", rows_in, first_grad, preferred_element_type=jnp.float32)
    ).astype(jnp.bfloat16)
    rows_total, cols_total = lax.psum((rows_sum, cols_sum), ("dp", "seq", "chan"))
    gate_blocks_total, up_blocks_total, gate_mix_total, up_mix_total = lax.psum(
        (blocks_gate_sum, blocks_up_sum, mix_gate_sum, mix_up_sum), ("dp", "seq")
    )
    count_dp = lax.axis_size("dp")
    count_seq = lax.axis_size("seq")
    count_chan = lax.axis_size("chan")
    batch_all = batch_dev * count_dp
    rows_all = rows_dev * count_seq
    width_all = width_dev * count_chan
    rows_scale = 1.0 / math.sqrt(batch_all * rows_all * width_all)
    cols_scale = 1.0 / math.sqrt(batch_all * cols_all * width_all)
    block_scale = 1.0 / math.sqrt(batch_all * rows_all * cols_all)
    return (
        input_grad,
        rows_total * rows_scale,
        cols_total * cols_scale,
        gate_blocks_total * block_scale,
        up_blocks_total * block_scale,
        gate_mix_total * block_scale,
        up_mix_total * block_scale,
    )


def solution(mesh):
    in_specs = (
        P("dp", "seq", None, "chan"),
        P("dp", "seq", None, "chan"),
        P(),
        P(),
        P("chan", None, None),
        P("chan", None, None),
        P(),
        P(),
    )
    out_specs = (
        P("dp", "seq", None, "chan"),
        P(),
        P(),
        P("chan", None, None),
        P("chan", None, None),
        P(None, "chan", None),
        P(None, "chan", None),
    )
    return jax.shard_map(body, mesh=mesh, in_specs=in_specs, out_specs=out_specs, check_vma=False)
```

profile of v0, /device:TPU:0, one launch (start us, length us, event | category | flops | bytes accessed | tf_op | source)
XLA Modules:
  0.0 618.1 jit_solution(10451862501799467449)
XLA Ops:
  10.1 31.8 %all_to_all.54 = bf16[1,2,256,1024]{3,1,0,2:T(2,128)(2,1)S(1)} all-to-all(bf16[1,2,256,1024]{3,1,0,2:T(2,128)(2,1)S(1)} %copy.163), channel_id=1, replica_groups=mesh['dp'=4,'seq'=4,'chan'=2] {'seq'}, dimensions={2} | all-to-all | bytes 2097152 | tf_op jit(solution)/shard_map/all_to_all | solution.py:25
  44.9 27.8 %all_to_all.55 = bf16[1,8,64,1024]{3,2,0,1:T(8,128)(2,1)S(1)} all-to-all(bf16[1,8,64,1024]{3,2,0,1:T(8,128)(2,1)S(1)} %copy.166), channel_id=1, replica_groups=mesh['dp'=4,'seq'=4,'chan'=2] {'seq'}, dimensions={1} | all-to-all | bytes 2097152 | tf_op jit(solution)/shard_map/all_to_all | solution.py:27
  88.8 26.0 %all-gather.5.cloned.1.call-done = bf16[1,2,256,4,512]{4,2,1,0,3:T(8,128)(2,1)} async-done(((bf16[1,2,256,2,512]{4,2,1,0,3:T(8,128)(2,1)}), bf16[1,2,256,4,512]{4,2,1,0,3:T(8,128)(2,1)}) %all-gather.5.cloned.1.call-update) | async-done | bytes 2097168 | tf_op jit(solution)/shard_map/all_gather | solution.py:50
  114.8 4.5 copy.170
  119.3 4.2 fusion.14
  123.5 4.2 copy.172
  127.7 22.4 %all-gather.7.cloned.1.call-done = bf16[1,2,256,4,512]{4,2,1,0,3:T(8,128)(2,1)} async-done(((bf16[1,2,256,2,512]{4,2,1,0,3:T(8,128)(2,1)}), bf16[1,2,256,4,512]{4,2,1,0,3:T(8,128)(2,1)}) %all-gather.7.cloned.1.call-update) | async-done | bytes 2097168 | tf_op jit(solution)/shard_map/all_gather | solution.py:45
  150.1 4.5 copy.176
  154.6 4.1 fusion.12
  158.7 4.1 copy.178
  162.9 5.0 fusion.10
  173.4 28.8 %all-gather.11.cloned.1.call-done = bf16[1,2,256,4,512]{4,2,1,0,3:T(8,128)(2,1)} async-done(((bf16[1,2,256,2,512]{4,2,1,0,3:T(8,128)(2,1)}), bf16[1,2,256,4,512]{4,2,1,0,3:T(8,128)(2,1)}) %all-gather.11.cloned.1.call-update) | async-done | bytes 2097168 | tf_op jit(solution)/shard_map/all_gather | solution.py:58
  202.2 4.5 copy.186
  206.7 3.9 fusion.30
  213.1 24.3 %all-gather.9.cloned.1.call-done = bf16[1,2,256,4,512]{4,2,1,0,3:T(8,128)(2,1)} async-done(((bf16[1,2,256,2,512]{4,2,1,0,3:T(8,128)(2,1)}), bf16[1,2,256,4,512]{4,2,1,0,3:T(8,128)(2,1)}) %all-gather.9.cloned.1.call-update) | async-done | bytes 2097168 | tf_op jit(solution)/shard_map/all_gather | solution.py:57
  237.3 4.5 copy.180
  254.9 4.6 all-to-all-start.2
  269.1 23.6 %all-to-all-done.2 = bf16[1,2,256,1024]{3,1,0,2:T(2,128)(2,1)} async-done(((bf16[1,2,256,1024]{3,1,0,2:T(2,128)(2,1)}), bf16[1,2,256,1024]{3,1,0,2:T(2,128)(2,1)}, u32[]{:S(2)}, u32[]{:S(2)}) %all-to-all-start.2) | async-done | bytes 1048608 | tf_op jit(solution)/shard_map/all_to_all | solution.py:88
  297.8 4.3 all-to-all-start.3
  302.1 5.5 fusion.39
  311.1 120.2 %all-reduce = (f32[4,2,512]{0,1,2:T(2,128)}, f32[4,2,512]{0,1,2:T(2,128)}) all-reduce(f32[4,2,512]{0,1,2:T(2,128)} %fusion.39, f32[4,2,512]{0,1,2:T(2,128)} %fusion.42), channel_id=1, replica_groups=mesh['dp'=4,'seq'=4,'chan'=2] {'dp','seq'}, use_global_device_ids=true, to_apply=%region_4.0 | all-reduce | flops 8192 | bytes 65536 | tf_op jit(solution)/shard_map/psum | solution.py:100
  438.5 36.9 %psum.43 = f32[8,8]{1,0:T(8,128)S(1)} all-reduce(f32[8,8]{1,0:T(8,128)S(1)} %convolution_bitcast_fusion.3), channel_id=1, replica_groups=mesh['dp'=4,'seq'=4,'chan'=2] {'dp','seq','chan'}, use_global_device_ids=true, to_apply=%region_1.0 | all-reduce | flops 64 | bytes 512 | tf_op jit(solution)/shard_map/psum | solution.py:99
  475.9 4.7 broadcast_multiply_fusion
  487.2 122.4 %all-reduce.5.cloned.1.call-done = f32[256,256]{1,0:T(8,128)} async-done(((f32[256,256]{1,0:T(8,128)}), f32[256,256]{1,0:T(8,128)}) %all-reduce.5.cloned.1.call-update) | async-done | bytes 262160 | tf_op jit(solution)/shard_map/psum | solution.py:99
  (108 shorter events, 76.8 us)
Async XLA Ops:
  7.2 75.4 %copy-start = (bf16[2,512,512]{2,1,0:T(8,128)(2,1)S(1)}, bf16[2,512,512]{2,1,0:T(8,128)(2,1)}, u32[]{:S(2)}) copy-start(bf16[2,512,512]{2,1,0:T(8,128)(2,1)} %param.12) | copy-start | bytes 3145732
  7.2 107.7 %all-gather.5.cloned.1.call-start = ((), (), s32[]{:S(2)}) async-start(), calls=%async_computation.4 | async-start | bytes 3145728 | tf_op jit(solution)/shard_map/all_gather | solution.py:50
  42.3 1.6 copy-start.19
  75.5 5.1 copy-start.12
  82.4 2.1 copy-start.17
  82.5 3.0 copy-start.18
  82.5 67.6 %all-gather.7.cloned.1.call-start = ((), (), s32[]{:S(2)}) async-start(), calls=%async_computation.5 | async-start | bytes 3145728 | tf_op jit(solution)/shard_map/all_gather | solution.py:45
  84.3 117.9 %all-gather.11.cloned.1.call-start = ((), (), s32[]{:S(2)}) async-start(), calls=%async_computation.7 | async-start | bytes 3145728 | tf_op jit(solution)/shard_map/all_gather | solution.py:58
  168.9 68.4 %all-gather.9.cloned.1.call-start = ((), (), s32[]{:S(2)}) async-start(), calls=%async_computation.6 | async-start | bytes 3145728 | tf_op jit(solution)/shard_map/all_gather | solution.py:57
  213.0 38.4 %copy-start.6 = (bf16[2,256,2,512]{3,1,0,2:T(8,128)(2,1)}, bf16[2,256,2,512]{3,1,0,2:T(8,128)(2,1)S(1)}, u32[]{:S(2)}) copy-start(bf16[2,256,2,512]{3,1,0,2:T(8,128)(2,1)S(1)} %copy.188) | copy-start | bytes 3145732
  249.3 2.1 copy-start.11
  249.3 2.2 copy-start.13
  252.8 6.8 %copy-start.7 = (bf16[2,256,2,512]{3,1,0,2:T(8,128)(2,1)S(1)}, bf16[2,256,2,512]{3,1,0,2:T(8,128)(2,1)}, u32[]{:S(2)}) copy-start(bf16[2,256,2,512]{3,1,0,2:T(8,128)(2,1)} %copy-done.6) | copy-start | bytes 3145732
  254.9 37.7 %all-to-all-start.2 = ((bf16[1,2,256,1024]{3,1,0,2:T(2,128)(2,1)}), bf16[1,2,256,1024]{3,1,0,2:T(2,128)(2,1)}, u32[]{:S(2)}, u32[]{:S(2)}) async-start(bf16[1,2,256,1024]{3,1,0,2:T(2,128)(2,1)} %copy.190), calls=%async_computation.2 | async-start | bytes 2097152 | tf_op jit(solution)/shard_map/all_to_all | solution.py:88
  259.5 216.4 %all-reduce.7.cloned.1.call-start = ((), (), s32[]{:S(2)}) async-start(), calls=%async_computation.9 | async-start | bytes 8388608 | tf_op jit(solution)/shard_map/psum | solution.py:100
  259.6 2.0 copy-start.10
  263.7 3.3 copy-start.4
  297.8 182.9 %all-to-all-start.3 = ((bf16[1,8,64,1024]{3,2,0,1:T(8,128)(2,1)}), bf16[1,8,64,1024]{3,2,0,1:T(8,128)(2,1)}, u32[]{:S(2)}, u32[]{:S(2)}) async-start(bf16[1,8,64,1024]{3,2,0,1:T(8,128)(2,1)} %copy.194), calls=%async_computation.3 | async-start | bytes 2097152 | tf_op jit(solution)/shard_map/all_to_all | solution.py:93
  302.1 5.5 copy-start.15
  302.1 307.5 %all-reduce.5.cloned.1.call-start = ((), (), s32[]{:S(2)}) async-start(), calls=%async_computation.8 | async-start | bytes 524288 | tf_op jit(solution)/shard_map/psum | solution.py:99
  302.1 5.5 copy-start.14
  311.1 126.6 %copy-start.3 = (bf16[8,64,1024]{2,0,1:T(8,128)(2,1)S(1)}, bf16[8,64,1024]{2,0,1:T(8,128)(2,1)}, u32[]{:S(2)}) copy-start(bf16[8,64,1024]{2,0,1:T(8,128)(2,1)} %copy-done.2) | copy-start | bytes 3145732
  480.7 2.7 copy-start.16
  483.4 127.9 %copy-start.1 = (bf16[2,512,512]{2,1,0:T(8,128)(2,1)S(1)}, bf16[2,512,512]{2,1,0:T(8,128)(2,1)}, u32[]{:S(2)}) copy-start(bf16[2,512,512]{2,1,0:T(8,128)(2,1)} %param.12) | copy-start | bytes 3145732
  (4 other events, 5.0 us)
Sparse Core Ops, SparseCore 0:
  82.6 32.2 all-gather.4
  117.0 33.1 all-gather.6
  169.0 33.1 all-gather.10
  204.2 33.1 all-gather.8
  264.4 161.0 all-reduce.6
  483.5 126.0 all-reduce.4
where the time goes:
time: 620 us; the launch traced here: 618 us
  waiting for transfers between devices  248 us (40%)
  blocking collectives  217 us (35%)
  local copies, waits for them, and re-layouts  72.1 us (12%)
  matrix products  41.5 us (7%)
  other arithmetic  16.3 us (3%)
  between operations  14.5 us (2%)
  starting transfers between devices  9.24 us (1%)
    psum x1, waiting for transfers between devices, body(): lax.psum((rows_sum, cols_sum), ('dp', 'seq', 'chan'))  122 us
    psum x1, blocking collectives, body(): lax.psum((blocks_gate_sum, blocks_up_sum, mix_gate_sum, mix_up_sum), ('dp...  120 us
    psum x1, blocking collectives, body(): lax.psum((rows_sum, cols_sum), ('dp', 'seq', 'chan'))  36.9 us
    all_to_all x1, blocking collectives, body(): lax.all_to_all(first, 'seq', split_axis=2, concat_axis=1, tiled=True)  31.8 us
    all_gather x1, waiting for transfers between devices, body(): lax.all_gather(up_grad, 'chan', axis=3, tiled=True)  28.8 us
    all_to_all x1, blocking collectives, body(): lax.all_to_all(second_cols, 'seq', split_axis=1, concat_axis=2, tiled=True)  27.8 us
    all_gather x1, waiting for transfers between devices, body(): lax.all_gather(up_mid, 'chan', axis=3, tiled=True).astype(jnp.float32)  26 us
    all_gather x1, waiting for transfers between devices, body(): lax.all_gather(gate_grad, 'chan', axis=3, tiled=True)  24.3 us
  transfers between devices with their start and end apart: 8, of which 6 were waited for; matrix products, arithmetic and copies ran while one was open for 12% of the time, Pallas kernels for 0%

commit v1 on v0

--- a/solution.py
+++ b/solution.py
@@ -3,6 +3,7 @@
 import jax.numpy as jnp
 from jax import lax
 from jax.sharding import PartitionSpec as P
+from jax.lax import psum
 
 
 def column_keep(segment, cols_mix):
@@ -97,8 +98,9 @@
         + jnp.einsum("ec,bred->brcd", rows_in, first_grad, preferred_element_type=jnp.float32)
     ).astype(jnp.bfloat16)
     rows_total, cols_total = lax.psum((rows_sum, cols_sum), ("dp", "seq", "chan"))
-    gate_blocks_total, up_blocks_total, gate_mix_total, up_mix_total = lax.psum(
-        (blocks_gate_sum, blocks_up_sum, mix_gate_sum, mix_up_sum), ("dp", "seq")
+    gate_blocks_total, up_blocks_total, gate_mix_total, up_mix_total = psum(
+        psum((blocks_gate_sum, blocks_up_sum, mix_gate_sum, mix_up_sum), axis_name="seq"),
+        axis_name="dp",
     )
     count_dp = lax.axis_size("dp")
     count_seq = lax.axis_size("seq")

time: 620 us -> 685 us (1.10)
  blocking collectives: 217 us -> 278 us
  waiting for transfers between devices: 248 us -> 264 us
  starting transfers between devices: 9.24 us -> 0.69 us
    psum x1 -> x2, waiting for transfers between devices: 0.01 us -> 164 us  [the longest x1 85.6 us: body(): psum(psum((blocks_gate_sum, blocks_up_sum, mix_gate_sum, mix_up_sum), axi...]
    psum x1, waiting for transfers between devices: 122 us -> 0.09 us  [body(): lax.psum((rows_sum, cols_sum), ('dp', 'seq', 'chan'))]
    all_to_all x0 -> x2, blocking collectives: none -> 108 us  [the longest x1 58.1 us: body(): lax.all_to_all(hidden_grad, 'seq', split_axis=2, concat_axis=1, tiled=True)]
    psum x1 -> x2, blocking collectives: 120 us -> 69.9 us  [the longest x1 43.2 us: body(): psum((blocks_gate_sum, blocks_up_sum, mix_gate_sum, mix_up_sum), axis_nam...]
    all_to_all x2 -> x0, waiting for transfers between devices: 23.6 us -> none  [the longest x1 23.6 us: body(): lax.all_to_all(hidden_grad, 'seq', split_axis=2, concat_axis=1, tiled=True)]
    all_to_all x2 -> x0, starting transfers between devices: 8.85 us -> none  [the longest x1 4.6 us: body(): lax.all_to_all(hidden_grad, 'seq', split_axis=2, concat_axis=1, tiled=True)]
  transfers between devices with their start and end apart: 8 -> 7, of which waited for: 6 -> 7; matrix products, arithmetic and copies ran while one was open for 12% -> 10% of each run, Pallas kernels for 0% -> 0%
where the time goes in v1:
time: 685 us; the launch traced here: 684 us
  blocking collectives  278 us (41%)
  waiting for transfers between devices  264 us (39%)
  local copies, waits for them, and re-layouts  68.6 us (10%)
  matrix products  43.2 us (6%)
  other arithmetic  15.2 us (2%)
  between operations  14.5 us (2%)
    psum x1, waiting for transfers between devices, body(): psum(psum((blocks_gate_sum, blocks_up_sum, mix_gate_sum, mix_up_sum), axi...  85.6 us
    psum x1, waiting for transfers between devices, body(): psum((blocks_gate_sum, blocks_up_sum, mix_gate_sum, mix_up_sum), axis_nam...  78.7 us
    all_to_all x1, blocking collectives, body(): lax.all_to_all(hidden_grad, 'seq', split_axis=2, concat_axis=1, tiled=True)  58.1 us
    all_to_all x1, blocking collectives, body(): lax.all_to_all(mixed, 'seq', split_axis=1, concat_axis=2, tiled=True)  50.1 us
    psum x1, blocking collectives, body(): psum((blocks_gate_sum, blocks_up_sum, mix_gate_sum, mix_up_sum), axis_nam...  43.2 us
    psum x1, blocking collectives, body(): lax.psum((rows_sum, cols_sum), ('dp', 'seq', 'chan'))  39.9 us
    all_to_all x1, blocking collectives, body(): lax.all_to_all(first, 'seq', split_axis=2, concat_axis=1, tiled=True)  31.8 us
    all_gather x1, waiting for transfers between devices, body(): lax.all_gather(up_grad, 'chan', axis=3, tiled=True)  28.8 us
  transfers between devices with their start and end apart: 7, of which 7 were waited for; matrix products, arithmetic and copies ran while one was open for 10% of the time, Pallas kernels for 0%

profile of v1, /device:TPU:0, one launch (start us, length us, event | category | flops | bytes accessed | tf_op | source)
XLA Modules:
  0.0 683.6 jit_solution(17059473160936973338)
XLA Ops:
  10.1 31.8 %all_to_all.54 = bf16[1,2,256,1024]{3,1,0,2:T(2,128)(2,1)S(1)} all-to-all(bf16[1,2,256,1024]{3,1,0,2:T(2,128)(2,1)S(1)} %copy.163), channel_id=1, replica_groups=mesh['dp'=4,'seq'=4,'chan'=2] {'seq'}, dimensions={2} | all-to-all | bytes 2097152 | tf_op jit(solution)/shard_map/all_to_all | solution.py:26
  44.9 27.8 %all_to_all.55 = bf16[1,8,64,1024]{3,2,0,1:T(8,128)(2,1)S(1)} all-to-all(bf16[1,8,64,1024]{3,2,0,1:T(8,128)(2,1)S(1)} %copy.166), channel_id=1, replica_groups=mesh['dp'=4,'seq'=4,'chan'=2] {'seq'}, dimensions={1} | all-to-all | bytes 2097152 | tf_op jit(solution)/shard_map/all_to_all | solution.py:28
  86.7 26.0 %all-gather.5.cloned.1.call-done = bf16[1,2,256,4,512]{4,2,1,0,3:T(8,128)(2,1)} async-done(((bf16[1,2,256,2,512]{4,2,1,0,3:T(8,128)(2,1)}), bf16[1,2,256,4,512]{4,2,1,0,3:T(8,128)(2,1)}) %all-gather.5.cloned.1.call-update) | async-done | bytes 2097168 | tf_op jit(solution)/shard_map/all_gather | solution.py:51
  112.7 4.5 copy.170
  117.2 4.2 fusion.14
  121.4 4.3 copy.172
  125.7 22.3 %all-gather.7.cloned.1.call-done = bf16[1,2,256,4,512]{4,2,1,0,3:T(8,128)(2,1)} async-done(((bf16[1,2,256,2,512]{4,2,1,0,3:T(8,128)(2,1)}), bf16[1,2,256,4,512]{4,2,1,0,3:T(8,128)(2,1)}) %all-gather.7.cloned.1.call-update) | async-done | bytes 2097168 | tf_op jit(solution)/shard_map/all_gather | solution.py:46
  148.0 4.5 copy.176
  152.5 4.1 fusion.12
  156.6 4.1 copy.178
  160.8 5.0 fusion.10
  171.3 28.8 %all-gather.11.cloned.1.call-done = bf16[1,2,256,4,512]{4,2,1,0,3:T(8,128)(2,1)} async-done(((bf16[1,2,256,2,512]{4,2,1,0,3:T(8,128)(2,1)}), bf16[1,2,256,4,512]{4,2,1,0,3:T(8,128)(2,1)}) %all-gather.11.cloned.1.call-update) | async-done | bytes 2097168 | tf_op jit(solution)/shard_map/all_gather | solution.py:59
  200.1 4.5 copy.186
  213.1 22.2 %all-gather.9.cloned.1.call-done = bf16[1,2,256,4,512]{4,2,1,0,3:T(8,128)(2,1)} async-done(((bf16[1,2,256,2,512]{4,2,1,0,3:T(8,128)(2,1)}), bf16[1,2,256,4,512]{4,2,1,0,3:T(8,128)(2,1)}) %all-gather.9.cloned.1.call-update) | async-done | bytes 2097168 | tf_op jit(solution)/shard_map/all_gather | solution.py:58
  235.2 4.5 copy.180
  258.3 58.1 %all_to_all.56 = bf16[1,2,256,1024]{3,1,0,2:T(2,128)(2,1)S(1)} all-to-all(bf16[1,2,256,1024]{3,1,0,2:T(2,128)(2,1)S(1)} %copy.190), channel_id=1, replica_groups=mesh['dp'=4,'seq'=4,'chan'=2] {'seq'}, dimensions={2} | all-to-all | bytes 2097152 | tf_op jit(solution)/shard_map/all_to_all | solution.py:89
  319.3 50.1 %all_to_all.57 = bf16[1,8,64,1024]{3,2,0,1:T(8,128)(2,1)S(1)} all-to-all(bf16[1,8,64,1024]{3,2,0,1:T(8,128)(2,1)S(1)} %copy.194), channel_id=1, replica_groups=mesh['dp'=4,'seq'=4,'chan'=2] {'seq'}, dimensions={1} | all-to-all | bytes 2097152 | tf_op jit(solution)/shard_map/all_to_all | solution.py:94
  371.8 78.7 %all-reduce.10.cloned.1.call-done = (f32[2,512,512]{2,1,0:T(8,128)}, f32[2,512,512]{2,1,0:T(8,128)}) async-done(((f32[2,512,512]{2,1,0:T(8,128)}, f32[2,512,512]{2,1,0:T(8,128)}), (f32[2,512,512]{2,1,0:T(8,128)}, f32[2,512,512]{2,1,0:T(8,128)})) %all-reduce.10.cloned.1.call-update) | async-done | bytes 4194320 | tf_op jit(solution)/shard_map/psum | solution.py:102
  454.8 4.6 fusion.39
  462.9 43.2 %all-reduce = (f32[4,2,512]{0,1,2:T(2,128)S(1)}, f32[4,2,512]{0,1,2:T(2,128)}) all-reduce(f32[4,2,512]{0,1,2:T(2,128)S(1)} %fusion.39, f32[4,2,512]{0,1,2:T(2,128)} %fusion.42), channel_id=1, replica_groups=mesh['dp'=4,'seq'=4,'chan'=2] {'seq'}, use_global_device_ids=true, to_apply=%region_6.0 | all-reduce | flops 8192 | bytes 65536 | tf_op jit(solution)/shard_map/psum | solution.py:102
  506.1 26.7 %all-reduce.2 = (f32[4,2,512]{0,1,2:T(2,128)S(1)}, f32[4,2,512]{0,1,2:T(2,128)}) all-reduce(f32[4,2,512]{0,1,2:T(2,128)S(1)} %get-tuple-element.42, f32[4,2,512]{0,1,2:T(2,128)} %get-tuple-element.43), channel_id=1, replica_groups=mesh['dp'=4,'seq'=4,'chan'=2] {'dp'}, use_global_device_ids=true, to_apply=%region_7.0 | all-reduce | flops 8192 | bytes 65536 | tf_op jit(solution)/shard_map/psum | solution.py:101
  541.1 39.9 %psum.71 = f32[8,8]{1,0:T(8,128)S(1)} all-reduce(f32[8,8]{1,0:T(8,128)S(1)} %convolution_bitcast_fusion.3), channel_id=1, replica_groups=mesh['dp'=4,'seq'=4,'chan'=2] {'dp','seq','chan'}, use_global_device_ids=true, to_apply=%region_1.0 | all-reduce | flops 64 | bytes 512 | tf_op jit(solution)/shard_map/psum | solution.py:100
  586.4 85.6 %all-reduce.12.cloned.1.call-done = (f32[2,512,512]{2,1,0:T(8,128)}, f32[2,512,512]{2,1,0:T(8,128)}) async-done(((f32[2,512,512]{2,1,0:T(8,128)}, f32[2,512,512]{2,1,0:T(8,128)}), (f32[2,512,512]{2,1,0:T(8,128)}, f32[2,512,512]{2,1,0:T(8,128)})) %all-reduce.12.cloned.1.call-update) | async-done | bytes 4194320 | tf_op jit(solution)/shard_map/psum | solution.py:101
  672.0 4.7 broadcast_multiply_fusion
  (110 shorter events, 78.7 us)
Async XLA Ops:
  7.2 73.3 %copy-start = (bf16[2,512,512]{2,1,0:T(8,128)(2,1)S(1)}, bf16[2,512,512]{2,1,0:T(8,128)(2,1)}, u32[]{:S(2)}) copy-start(bf16[2,512,512]{2,1,0:T(8,128)(2,1)} %param.12) | copy-start | bytes 3145732
  7.2 105.6 %all-gather.5.cloned.1.call-start = ((), (), s32[]{:S(2)}) async-start(), calls=%async_computation.4 | async-start | bytes 3145728 | tf_op jit(solution)/shard_map/all_gather | solution.py:51
  42.3 1.6 copy-start.19
  72.9 1.2 copy-start.9
  74.5 4.0 copy-start.13
  80.3 2.1 copy-start.17
  80.4 3.0 copy-start.18
  80.4 67.6 %all-gather.7.cloned.1.call-start = ((), (), s32[]{:S(2)}) async-start(), calls=%async_computation.5 | async-start | bytes 3145728 | tf_op jit(solution)/shard_map/all_gather | solution.py:46
  82.2 117.9 %all-gather.11.cloned.1.call-start = ((), (), s32[]{:S(2)}) async-start(), calls=%async_computation.7 | async-start | bytes 3145728 | tf_op jit(solution)/shard_map/all_gather | solution.py:59
  166.8 68.4 %all-gather.9.cloned.1.call-start = ((), (), s32[]{:S(2)}) async-start(), calls=%async_computation.6 | async-start | bytes 3145728 | tf_op jit(solution)/shard_map/all_gather | solution.py:58
  169.2 281.3 %all-reduce.10.cloned.1.call-start = ((), (), s32[]{:S(2)}) async-start(), calls=%async_computation.9 | async-start | bytes 8388608 | tf_op jit(solution)/shard_map/psum | solution.py:102
  250.6 1.2 copy-start.11
  250.6 334.1 %all-reduce.8.cloned.1.call-start = ((), (), s32[]{:S(2)}) async-start(), calls=%async_computation.8 | async-start | bytes 524288 | tf_op jit(solution)/shard_map/psum | solution.py:100
  251.8 1.6 copy-start.12
  251.8 1.9 copy-start.14
  257.1 59.2 %copy-start.5 = (bf16[1,2,256,2,512]{2,4,3,1,0:T(8,128)(2,1)}, bf16[1,2,256,2,512]{2,4,3,1,0:T(8,128)(2,1)S(1)}, u32[]{:S(2)}) copy-start(bf16[1,2,256,2,512]{2,4,3,1,0:T(8,128)(2,1)S(1)} %copy.189) | copy-start | bytes 3145732
  319.3 51.2 %copy-start.10 = (bf16[1,2,256,1024]{3,2,1,0:T(8,128)(2,1)S(1)}, bf16[1,2,256,1024]{3,2,1,0:T(8,128)(2,1)}, u32[]{:S(2)}) copy-start(bf16[1,2,256,1024]{3,2,1,0:T(8,128)(2,1)} %param.8) | copy-start | bytes 3145732
  371.7 300.3 %all-reduce.12.cloned.1.call-start = ((), (), s32[]{:S(2)}) async-start(), calls=%async_computation.10 | async-start | bytes 8388608 | tf_op jit(solution)/shard_map/psum | solution.py:101
  450.5 1.2 copy-start.4
  450.5 3.3 copy-start.3
  454.8 4.6 copy-start.15
  506.0 33.0 %copy-start.2 = (bf16[8,64,1024]{2,0,1:T(8,128)(2,1)S(1)}, bf16[8,64,1024]{2,0,1:T(8,128)(2,1)}, u32[]{:S(2)}) copy-start(bf16[8,64,1024]{2,0,1:T(8,128)(2,1)} %copy-done.1) | copy-start | bytes 3145732
  535.3 46.3 %copy-start.6 = (bf16[1,2,256,2,512]{2,4,3,1,0:T(8,128)(2,1)S(1)}, bf16[1,2,256,2,512]{2,4,3,1,0:T(8,128)(2,1)}, u32[]{:S(2)}) copy-start(bf16[1,2,256,2,512]{2,4,3,1,0:T(8,128)(2,1)} %copy-done.5) | copy-start | bytes 3145732
  535.3 46.3 %copy-start.16 = (bf16[256,256]{1,0:T(8,128)(2,1)S(1)}, bf16[256,256]{1,0:T(8,128)(2,1)}, u32[]{:S(2)}) copy-start(bf16[256,256]{1,0:T(8,128)(2,1)} %param.10) | copy-start | bytes 393220
  (3 other events, 3.1 us)
Sparse Core Ops, SparseCore 0:
  80.5 32.2 all-gather.4
  114.8 33.1 all-gather.6
  166.9 33.1 all-gather.10
  202.1 33.1 all-gather.8
  250.7 199.7 all-reduce.9
  457.3 127.3 all-reduce.7
  587.3 84.6 all-reduce.11
